TPU v7x, 256 devices: a whole 4x4x8 slice. The times are simulated.
256 devices in a mesh: clus: 4 (over z_lo, core), sub: 64 (over x, z_hi, y).
Axes of the slice: x: 4, y: 4, z: 8 (z_hi: 4, z_lo: 2; z = z_hi * 2 + z_lo), core: 2. Of those that a mesh axis runs over, the one named last changes fastest.
Arguments:
- load: float32 [4, 64, 6, 256, 128], P('clus', 'sub'), may hold values from -30 to 30
- dual_op: float32 [4, 64, 1536, 1536], P('clus', 'sub'), may hold values from -6 to 17, as said below
- modes: float32 [4, 64, 32, 1536], P('clus', 'sub'), may hold values from -1 to 1
- face_map: int32 [4, 64, 3, 256], P('clus', 'sub'), may hold values from 0 to 255, each once within a row
- cluster: int32 [4, 64], P('clus', 'sub'), may hold values from 0 to 1, as said below
Outputs:
- multipliers: float32 [4, 64, 6, 256, 128], P('clus', 'sub')
- residual: float32 [4, 64, 6, 256, 128], P('clus', 'sub')
Inputs may be any that keep to these rules, and one draw needn't show every extreme that they name: `dual_op`: each subdomain's block is symmetric positive definite. `face_map`: each row of 256 entries names every row of the neighbour's face once. In every cluster group exactly half of the 64 subdomains belong to each of its two clusters.
All inputs are finite; a program needn't handle non-finite values.
Results may differ from a plain program's by a relative error of at most 0.00011.
Values sent between devices are 32-bit elements; how exact they have to be, the bound alone decides.
No kernel may reach another device: no remote copies, remote signals or barrier semaphores. Data moves between devices by JAX's collectives and lax.ppermute only.
A program may use at most 128 MiB of HBM per device.

v0:
```python
import jax
import jax.numpy as jnp
from jax import lax
from jax.sharding import PartitionSpec as P

FACE = 256
COLS = 128
ITERS = 3
ORDER = 1536
damping_factor = 0.8
highest = lax.Precision.HIGHEST


def with_halo(cells, sides, width):
    for axis, dim in sides:
        count = lax.axis_size(axis)
        head = lax.slice_in_dim(cells, 0, width, axis=dim)
        tail = lax.slice_in_dim(cells, cells.shape[dim] - width, cells.shape[dim], axis=dim)
        cells = jnp.concatenate(
            [
                lax.ppermute(tail, axis, [(i, (i + 1) % count) for i in range(count)]),
                cells,
                lax.ppermute(head, axis, [((i + 1) % count, i) for i in range(count)]),
            ],
            axis=dim,
        )
    return cells


def from_partner(array, axis, distance):
    return lax.ppermute(array, axis, [(i, i ^ 1 << distance) for i in range(lax.axis_size(axis))])


def partner_values(values, pairing, inverse):
    result = []
    for direction in range(3):
        plus_face = values[2 * direction]
        minus_face = values[2 * direction + 1]
        upward = jnp.take(plus_face, inverse[direction], axis=0)
        width = upward.shape[0]
        if direction == 0:
            arrived = with_halo(jnp.concatenate([minus_face, upward], axis=0), (("sub", 0),), width)
            from_minus = arrived[:width]
            from_plus = arrived[3 * width :]
        elif direction == 1:
            arrived = with_halo(
                jnp.concatenate([minus_face, upward], axis=0), (("clus", 0),), width
            )
            from_minus = arrived[:width]
            from_plus = arrived[3 * width :]
        else:
            bit_index = lax.axis_size("sub").bit_length() - 2
            arrived = from_partner(jnp.stack([upward, minus_face]), "sub", bit_index)
            from_minus = arrived[0]
            from_plus = arrived[1]
        plus_side = jnp.take(from_plus, pairing[direction], axis=0)
        result += [plus_side, from_minus]
    return jnp.stack(result)


def solve_one(lower_part, column_block):
    return jax.scipy.linalg.cho_solve((lower_part, True), column_block)


def per_device(load, dual_op, modes, face_map, cluster):
    values = load[0, 0]
    operator = dual_op[0, 0]
    mode_rows = modes[0, 0]
    pairing = face_map[0, 0]
    member = cluster[0, 0]
    inverse = jnp.argsort(pairing, axis=-1)
    plus_owned = pairing % 2 == 0
    minus_owned = jnp.broadcast_to(jnp.arange(FACE) % 2 == 1, plus_owned.shape)
    owned = jnp.stack([plus_owned, minus_owned], axis=1).reshape(6, FACE, 1).astype(jnp.float32)
    selector = (jnp.arange(2) == member).astype(jnp.float32)
    weighted = mode_rows * owned.reshape(1, ORDER)
    gram_terms = jnp.einsum("mn,kn->mk", weighted, mode_rows, precision=highest)
    gram_total = lax.psum(selector[:, None, None] * gram_terms[None], "sub")
    factor = jnp.linalg.cholesky(gram_total)
    residual = values * owned
    multipliers = jnp.zeros_like(values)
    for iteration in range(ITERS):
        projected = jnp.einsum(
            "mn,nc->mc", mode_rows, residual.reshape(ORDER, COLS), precision=highest
        )
        gathered = lax.psum(selector[:, None, None] * projected[None], "sub")
        coefficients = jax.vmap(solve_one)(factor, gathered)
        own_coeff = lax.dynamic_index_in_dim(coefficients, member, 0, keepdims=False)
        correction = jnp.einsum("mn,mc->nc", mode_rows, own_coeff, precision=highest).reshape(
            6, FACE, COLS
        )
        search = residual - owned * correction
        local_copy = search - (1.0 - owned) * partner_values(search, pairing, inverse)
        applied = jnp.dot(operator, local_copy.reshape(ORDER, COLS), precision=highest).reshape(
            6, FACE, COLS
        )
        assembled = owned * (applied - partner_values(applied, pairing, inverse))
        numerator, denominator = lax.psum(
            (jnp.sum(residual * search, axis=(0, 1)), jnp.sum(search * assembled, axis=(0, 1))),
            ("clus", "sub"),
        )
        step_size = damping_factor * numerator / denominator
        multipliers = multipliers + step_size * search
        residual = residual - step_size * assembled
    return (multipliers[None, None], residual[None, None])


def solution(mesh):
    placed = (
        P("clus", "sub", None, None, None),
        P("clus", "sub", None, None),
        P("clus", "sub", None, None),
        P("clus", "sub", None, None),
        P("clus", "sub"),
    )
    return jax.shard_map(
        per_device,
        mesh=mesh,
        in_specs=placed,
        out_specs=(P("clus", "sub", None, None, None), P("clus", "sub", None, None, None)),
        check_vma=False,
    )
```

profile of v0, /device:TPU:1, one launch (start us, length us, event | category | flops | bytes accessed | tf_op | source)
XLA Modules:
  0.0 1692.0 jit_solution(10219532640262902524)
XLA Ops:
  22.2 326.7 %all-reduce.3 = (f32[2,32,128]{2,1,0:T(8,128)S(1)}, f32[2,32,32]{1,2,0:T(8,128)S(1)}) all-reduce(f32[2,32,128]{2,1,0:T(8,128)S(1)} %broadcast_multiply_fusion.3, f32[2,32,32]{1,2,0:T(8,128)S(1)} %broadcast_multiply_fusion.4), channel_id=1, replica_groups=mesh['clus'=4,'sub'=64] {'sub'}, use_global_device_ids=true, to_apply=%region_3.4 | all-reduce | flops 10240 | bytes 81920 | tf_op jit(solution)/shard_map/psum | solution.py:86
  349.0 5.9 custom-call.9
  355.1 4.9 custom-call.12
  373.3 56.8 %collective-permute-start.3 = (f32[256,128]{0,1:T(8,128)}, f32[256,128]{0,1:T(8,128)}, u32[]{:S(2)}, u32[]{:S(2)}) collective-permute-start(f32[256,128]{0,1:T(8,128)} %broadcast_select_fusion.10), channel_id=1, source_target_pairs={{0,64},{64,128},{128,192},{192,0},{1,65},{65,129},{129,193},{193,1... | collective-permute-start | bytes 393224 | tf_op jit(solution)/shard_map/ppermute | solution.py:21
  430.1 8.1 collective-permute-start
  439.5 3.8 collective-permute-done
  454.5 12.2 fusion.6
  472.0 8.7 collective-permute-start.5
  487.9 7.4 collective-permute-done.6
  500.7 77.2 %all-reduce.2 = (f32[128]{0:T(128)S(1)}, f32[128]{0:T(128)S(1)}) all-reduce(f32[128]{0:T(128)S(1)} %get-tuple-element.13, f32[128]{0:T(128)S(1)} %get-tuple-element.12), channel_id=1, replica_groups=mesh['clus'=4,'sub'=64] {'clus','sub'}, use_global_device_ids=true, to_apply=%region_8.11 | all-reduce | flops 256 | bytes 2048 | tf_op jit(solution)/shard_map/psum | solution.py:98
  581.6 316.0 %psum.74 = f32[2,32,128]{2,1,0:T(8,128)S(1)} all-reduce(f32[2,32,128]{2,1,0:T(8,128)S(1)} %broadcast_multiply_fusion.2), channel_id=1, replica_groups=mesh['clus'=4,'sub'=64] {'sub'}, use_global_device_ids=true, to_apply=%region_9.12 | all-reduce | flops 8192 | bytes 65536 | tf_op jit(solution)/shard_map/psum | solution.py:86
  913.0 56.4 %collective-permute-start.12 = (f32[256,128]{0,1:T(8,128)}, f32[256,128]{0,1:T(8,128)S(1)}, u32[]{:S(2)}, u32[]{:S(2)}) collective-permute-start(f32[256,128]{0,1:T(8,128)} %get-tuple-element.53), channel_id=1, source_target_pairs={{64,0},{128,64},{192,128},{0,192},{65,1},{129,65},{193,129},{1,193... | collective-permute-start | bytes 393224 | tf_op jit(solution)/shard_map/ppermute | solution.py:23
  994.1 12.1 fusion.9
  1013.1 4.6 collective-permute-start.15
  1046.2 77.9 %all-reduce.1 = (f32[128]{0:T(128)S(1)}, f32[128]{0:T(128)S(1)}) all-reduce(f32[128]{0:T(128)S(1)} %get-tuple-element.17, f32[128]{0:T(128)S(1)} %get-tuple-element.16), channel_id=1, replica_groups=mesh['clus'=4,'sub'=64] {'clus','sub'}, use_global_device_ids=true, to_apply=%region_13.16 | all-reduce | flops 256 | bytes 2048 | tf_op jit(solution)/shard_map/psum | solution.py:98
  1128.3 316.1 %psum.77 = f32[2,32,128]{2,1,0:T(8,128)S(1)} all-reduce(f32[2,32,128]{2,1,0:T(8,128)S(1)} %broadcast_multiply_fusion.1), channel_id=1, replica_groups=mesh['clus'=4,'sub'=64] {'sub'}, use_global_device_ids=true, to_apply=%region_14.17 | all-reduce | flops 8192 | bytes 65536 | tf_op jit(solution)/shard_map/psum | solution.py:86
  1448.0 2.8 multiply_subtract_fusion.2
  1456.7 56.1 %collective-permute-start.22 = (f32[256,128]{0,1:T(8,128)}, f32[256,128]{0,1:T(8,128)S(1)}, u32[]{:S(2)}, u32[]{:S(2)}) collective-permute-start(f32[256,128]{0,1:T(8,128)} %get-tuple-element.41), channel_id=1, source_target_pairs={{64,0},{128,64},{192,128},{0,192},{65,1},{129,65},{193,129},{1,193... | collective-permute-start | bytes 393224 | tf_op jit(solution)/shard_map/ppermute | solution.py:23
  1524.1 3.9 collective-permute-done.21
  1536.6 12.4 fusion.12
  1555.6 3.3 collective-permute-start.25
  1560.5 3.7 collective-permute-start.28
  1597.3 76.0 %all-reduce = (f32[128]{0:T(128)S(1)}, f32[128]{0:T(128)S(1)}) all-reduce(f32[128]{0:T(128)S(1)} %get-tuple-element.15, f32[128]{0:T(128)S(1)} %get-tuple-element.14), channel_id=1, replica_groups=mesh['clus'=4,'sub'=64] {'clus','sub'}, use_global_device_ids=true, to_apply=%region_18.21 | all-reduce | flops 256 | bytes 2048 | tf_op jit(solution)/shard_map/psum | solution.py:98
  1678.7 3.7 multiply_subtract_fusion
  (427 shorter events, 218.7 us)
Async XLA Ops:
  372.6 73.2 %collective-permute-start.1 = (f32[256,128]{0,1:T(8,128)}, f32[256,128]{0,1:T(8,128)}, u32[]{:S(2)}, u32[]{:S(2)}) collective-permute-start(f32[256,128]{0,1:T(8,128)} %broadcast_select_fusion.11), channel_id=1, source_target_pairs={{0,1},{1,2},{2,3},{3,4},{4,5},{5,6},{6,7},{7,8},{8,9},{9,10},{10,1... | collective-permute-start | bytes 393224 | tf_op jit(solution)/shard_map/ppermute | solution.py:21
  373.3 74.7 %collective-permute-start.3 = (f32[256,128]{0,1:T(8,128)}, f32[256,128]{0,1:T(8,128)}, u32[]{:S(2)}, u32[]{:S(2)}) collective-permute-start(f32[256,128]{0,1:T(8,128)} %broadcast_select_fusion.10), channel_id=1, source_target_pairs={{0,64},{64,128},{128,192},{192,0},{1,65},{65,129},{129,193},{193,1... | collective-permute-start | bytes 393224 | tf_op jit(solution)/shard_map/ppermute | solution.py:21
  430.1 13.2 collective-permute-start
  438.2 11.4 collective-permute-start.4
  470.5 14.9 collective-permute-start.7
  472.0 14.3 collective-permute-start.5
  484.0 11.3 collective-permute-start.6
  484.0 12.0 collective-permute-start.8
  485.4 10.6 collective-permute-start.9
  913.0 65.8 %collective-permute-start.12 = (f32[256,128]{0,1:T(8,128)}, f32[256,128]{0,1:T(8,128)S(1)}, u32[]{:S(2)}, u32[]{:S(2)}) collective-permute-start(f32[256,128]{0,1:T(8,128)} %get-tuple-element.53), channel_id=1, source_target_pairs={{64,0},{128,64},{192,128},{0,192},{65,1},{129,65},{193,129},{1,193... | collective-permute-start | bytes 393224 | tf_op jit(solution)/shard_map/ppermute | solution.py:23
  973.0 11.6 collective-permute-start.11
  974.5 11.1 collective-permute-start.13
  1011.5 13.1 collective-permute-start.17
  1013.1 13.3 collective-permute-start.15
  1021.1 10.8 collective-permute-start.16
  1021.1 12.4 collective-permute-start.18
  1456.7 63.8 %collective-permute-start.22 = (f32[256,128]{0,1:T(8,128)}, f32[256,128]{0,1:T(8,128)S(1)}, u32[]{:S(2)}, u32[]{:S(2)}) collective-permute-start(f32[256,128]{0,1:T(8,128)} %get-tuple-element.41), channel_id=1, source_target_pairs={{64,0},{128,64},{192,128},{0,192},{65,1},{129,65},{193,129},{1,193... | collective-permute-start | bytes 393224 | tf_op jit(solution)/shard_map/ppermute | solution.py:23
  1516.3 11.6 collective-permute-start.21
  1517.8 12.4 collective-permute-start.23
  1520.1 11.7 collective-permute-start.24
  1555.6 12.7 collective-permute-start.25
  1560.4 17.8 %collective-permute-start.26 = (f32[256,128]{0,1:T(8,128)}, f32[256,128]{0,1:T(8,128)}, u32[]{:S(2)}, u32[]{:S(2)}) collective-permute-start(f32[256,128]{0,1:T(8,128)} %broadcast_select_fusion.1), channel_id=1, source_target_pairs={{0,1},{1,2},{2,3},{3,4},{4,5},{5,6},{6,7},{7,8},{8,9},{9,10},{10,1... | collective-permute-start | bytes 393224 | tf_op jit(solution)/shard_map/ppermute | solution.py:21
  1560.5 23.9 %collective-permute-start.28 = (f32[256,128]{0,1:T(8,128)}, f32[256,128]{0,1:T(8,128)}, u32[]{:S(2)}, u32[]{:S(2)}) collective-permute-start(f32[256,128]{0,1:T(8,128)} %broadcast_select_fusion), channel_id=1, source_target_pairs={{0,64},{64,128},{128,192},{192,0},{1,65},{65,129},{129,193},{193,1... | collective-permute-start | bytes 393224 | tf_op jit(solution)/shard_map/ppermute | solution.py:21
  1565.9 24.8 %collective-permute-start.29 = (f32[2,256,128]{1,2,0:T(8,128)}, f32[2,256,128]{1,2,0:T(8,128)}, u32[]{:S(2)}, u32[]{:S(2)}) collective-permute-start(f32[2,256,128]{1,2,0:T(8,128)} %pad_maximum_fusion.5), channel_id=1, source_target_pairs={{0,32},{1,33},{2,34},{3,35},{4,36},{5,37},{6,38},{7,39},{8,40},{9,... | collective-permute-start | bytes 786440 | tf_op jit(solution)/shard_map/ppermute | solution.py:31
  (51 other events, 5264.2 us)
Sparse Core Ops, SparseCore 0:
  10.9 2.5 sort.21.cloned.1.call-done
  (1 shorter events, 0.0 us)
where the time goes:
time: 1700 us; the launch traced here: 1690 us
  blocking collectives  1190 us (70%)
  starting transfers between devices  212 us (12%)
  local copies, waits for them, and re-layouts  131 us (8%)
  other arithmetic  76 us (4%)
  matrix products  45.8 us (3%)
  waiting for transfers between devices  20.2 us (1%)
    psum x3, blocking collectives, per_device(): gathered = lax.psum(selector[:, None, None] * projected[None], 'sub')  959 us
    psum x3, blocking collectives, per_device(): lax.psum((jnp.sum(residual * search, axis=(0, 1)), jnp.sum(search * assem...  231 us
    ppermute x12, starting transfers between devices, with_halo(): lax.ppermute(head, axis, [((i + 1) % count, i) for i in range(count)])  140 us
    ppermute x12, starting transfers between devices, with_halo(): lax.ppermute(tail, axis, [(i, (i + 1) % count) for i in range(count)])  70.9 us
    dot_general x3, matrix products, per_device(): jnp.dot(operator, local_copy.reshape(ORDER, COLS), precision=highest)  36.7 us
  transfers between devices with their start and end apart: 30, of which 6 were waited for; matrix products, arithmetic and copies ran while one was open for 5% of the time, Pallas kernels for 0%

commit v1 on v0

--- a/solution.py
+++ b/solution.py
@@ -83,7 +83,7 @@
         projected = jnp.einsum(
             "mn,nc->mc", mode_rows, residual.reshape(ORDER, COLS), precision=highest
         )
-        gathered = lax.psum(selector[:, None, None] * projected[None], "sub")
+        gathered = jnp.sum(lax.all_gather(selector[:, None, None] * projected[None], "sub"), axis=0)
         coefficients = jax.vmap(solve_one)(factor, gathered)
         own_coeff = lax.dynamic_index_in_dim(coefficients, member, 0, keepdims=False)
         correction = jnp.einsum("mn,mc->nc", mode_rows, own_coeff, precision=highest).reshape(

time: 1700 us -> 1130 us (0.66)
  blocking collectives: 1190 us -> 557 us
  waiting for transfers between devices: 20.2 us -> 160 us
  starting transfers between devices: 212 us -> 109 us
    psum x3 -> x1, blocking collectives: 959 us -> 328 us  [per_device(): gram_total = lax.psum(selector[:, None, None] * gram_terms[None], 'sub')]
    all_gather x0 -> x3, waiting for transfers between devices: none -> 133 us  [per_device(): lax.all_gather(selector[:, None, None] * projected[None], 'sub')]
    ppermute x12, starting transfers between devices: 140 us -> 43.5 us  [with_halo(): lax.ppermute(head, axis, [((i + 1) % count, i) for i in range(count)])]
  transfers between devices with their start and end apart: 30 -> 33, of which waited for: 6 -> 7; matrix products, arithmetic and copies ran while one was open for 5% -> 9% of each run, Pallas kernels for 0% -> 0%
where the time goes in v1:
time: 1130 us; the launch traced here: 1120 us
  blocking collectives  557 us (49%)
  waiting for transfers between devices  160 us (14%)
  local copies, waits for them, and re-layouts  144 us (13%)
  starting transfers between devices  109 us (10%)
  other arithmetic  85.8 us (8%)
  matrix products  45.8 us (4%)
  between operations  16.4 us (1%)
    psum x1, blocking collectives, per_device(): gram_total = lax.psum(selector[:, None, None] * gram_terms[None], 'sub')  328 us
    psum x3, blocking collectives, per_device(): lax.psum((jnp.sum(residual * search, axis=(0, 1)), jnp.sum(search * assem...  229 us
    all_gather x3, waiting for transfers between devices, per_device(): lax.all_gather(selector[:, None, None] * projected[None], 'sub')  133 us
    ppermute x12, starting transfers between devices, with_halo(): lax.ppermute(tail, axis, [(i, (i + 1) % count) for i in range(count)])  63.4 us
    ppermute x12, starting transfers between devices, with_halo(): lax.ppermute(head, axis, [((i + 1) % count, i) for i in range(count)])  43.5 us
    dot_general x3, matrix products, per_device(): jnp.dot(operator, local_copy.reshape(ORDER, COLS), precision=highest)  36.7 us
    unnamed x99, local copies, waits for them, and re-layouts  32.3 us
    ppermute x12, waiting for transfers between devices, with_halo(): lax.ppermute(tail, axis, [(i, (i + 1) % count) for i in range(count)])  23.5 us
  transfers between devices with their start and end apart: 33, of which 7 were waited for; matrix products, arithmetic and copies ran while one was open for 9% of the time, Pallas kernels for 0%

profile of v1, /device:TPU:1, one launch (start us, length us, event | category | flops | bytes accessed | tf_op | source)
XLA Modules:
  0.0 1117.8 jit_solution(14273130519415006041)
XLA Ops:
  21.2 327.7 %psum.49 = f32[2,32,32]{1,2,0:T(8,128)S(1)} all-reduce(f32[2,32,32]{1,2,0:T(8,128)S(1)} %broadcast_multiply_fusion.4), channel_id=1, replica_groups=mesh['clus'=4,'sub'=64] {'sub'}, use_global_device_ids=true, to_apply=%region_0.0 | all-reduce | flops 2048 | bytes 16384 | tf_op jit(solution)/shard_map/psum | solution.py:78
  349.1 5.9 custom-call.9
  355.2 4.9 custom-call.12
  374.7 56.4 %collective-permute-start.3 = (f32[256,128]{0,1:T(8,128)}, f32[256,128]{0,1:T(8,128)}, u32[]{:S(2)}, u32[]{:S(2)}) collective-permute-start(f32[256,128]{0,1:T(8,128)} %broadcast_select_fusion.10), channel_id=1, source_target_pairs={{0,64},{64,128},{128,192},{192,0},{1,65},{65,129},{129,193},{193,1... | collective-permute-start | bytes 393224 | tf_op jit(solution)/shard_map/ppermute | solution.py:21
  431.1 8.1 collective-permute-start
  455.9 12.2 %fusion.6 = f32[1536,128]{0,1:T(8,128)S(1)} fusion(f32[1,1,1536,1536]{3,2,1,0:T(8,128)} %param.10, f32[1536,128]{0,1:T(8,128)S(1)} %copy.357, f32[1536,128]{0,1:T(8,128)} %copy-done.10, f32[1536,128]{0,1:T(8,128)S(1)} %copy.343, f32[1536]{0:T(1024)S(1)} %broadcast_subtract_fusion, f32[1536]{0:T(1024)S(1)} %reshape.635), kind=kOutput, calls=%fused_computation.45 | convolution fusion | flops 3624861696 | bytes 12595200 | tf_op jit(solution)/shard_map/dot_general | solution.py:94
  472.2 8.6 collective-permute-start.5
  487.6 6.7 collective-permute-done.6
  503.8 76.3 %all-reduce.2 = (f32[128]{0:T(128)S(1)}, f32[128]{0:T(128)S(1)}) all-reduce(f32[128]{0:T(128)} %get-tuple-element.15, f32[128]{0:T(128)} %get-tuple-element.14), channel_id=1, replica_groups=mesh['clus'=4,'sub'=64] {'clus','sub'}, use_global_device_ids=true, to_apply=%region_8.11 | all-reduce | flops 256 | bytes 2048 | tf_op jit(solution)/shard_map/psum | solution.py:98
  583.9 71.1 %all-gather.6.cloned.1.call-done = f32[64,2,32,128]{3,2,1,0:T(8,128)} async-done(((f32[1,2,32,128]{3,2,1,0:T(8,128)}), f32[64,2,32,128]{3,2,1,0:T(8,128)}) %all-gather.6.cloned.1.call-update) | async-done | bytes 2097168 | tf_op jit(solution)/shard_map/all_gather | solution.py:86
  674.7 6.0 collective-permute-start.10
  688.1 5.7 collective-permute-done.11
  704.4 12.1 %fusion.9 = f32[1536,128]{0,1:T(8,128)S(1)} fusion(f32[1,1,1536,1536]{3,2,1,0:T(8,128)} %param.10, f32[1536,128]{0,1:T(8,128)} %copy.393, f32[1536,128]{0,1:T(8,128)S(1)} %multiply_subtract_fusion.7, f32[1536,128]{0,1:T(8,128)S(1)} %copy-done.9, f32[1536]{0:T(1024)S(1)} %broadcast_subtract_fusion, f32[1536]{0:T(1024)S(1)} %reshape.635), kind=kOutput, calls=%fused_computation.46 | convolution fusion | flops 3624665088 | bytes 12595200 | tf_op jit(solution)/shard_map/dot_general | solution.py:94
  724.9 3.4 collective-permute-start.15
  739.1 3.9 collective-permute-done.16
  757.8 76.0 %all-reduce.1 = (f32[128]{0:T(128)}, f32[128]{0:T(128)}) all-reduce(f32[128]{0:T(128)} %get-tuple-element.19, f32[128]{0:T(128)} %get-tuple-element.18), channel_id=1, replica_groups=mesh['clus'=4,'sub'=64] {'clus','sub'}, use_global_device_ids=true, to_apply=%region_13.16 | all-reduce | flops 256 | bytes 2048 | tf_op jit(solution)/shard_map/psum | solution.py:98
  848.0 62.2 %all-gather.8.cloned.1.call-done = f32[64,2,32,128]{3,2,1,0:T(8,128)} async-done(((f32[1,2,32,128]{3,2,1,0:T(8,128)}), f32[64,2,32,128]{3,2,1,0:T(8,128)}) %all-gather.8.cloned.1.call-update) | async-done | bytes 2097168 | tf_op jit(solution)/shard_map/all_gather | solution.py:86
  924.8 3.1 collective-permute-start.22
  927.9 6.0 collective-permute-start.20
  942.1 7.2 collective-permute-done.21
  958.0 12.4 %fusion.12 = f32[1536,128]{0,1:T(8,128)S(1)} fusion(f32[1,1,1536,1536]{3,2,1,0:T(8,128)} %param.10, f32[1536,128]{0,1:T(8,128)} %copy.430, f32[1536,128]{0,1:T(8,128)} %copy-done.12, f32[1536,128]{0,1:T(8,128)S(1)} %copy-done.8, f32[1536]{0:T(1024)S(1)} %broadcast_subtract_fusion, f32[1536]{0:T(1024)S(1)} %reshape.635), kind=kOutput, calls=%fused_computation.47 | convolution fusion | flops 3624665088 | bytes 12595200 | tf_op jit(solution)/shard_map/dot_general | solution.py:94
  978.6 4.0 collective-permute-start.28
  1019.7 76.9 %all-reduce = (f32[128]{0:T(128)S(1)}, f32[128]{0:T(128)S(1)}) all-reduce(f32[128]{0:T(128)S(1)} %get-tuple-element.17, f32[128]{0:T(128)S(1)} %get-tuple-element.16), channel_id=1, replica_groups=mesh['clus'=4,'sub'=64] {'clus','sub'}, use_global_device_ids=true, to_apply=%region_18.21 | all-reduce | flops 256 | bytes 2048 | tf_op jit(solution)/shard_map/psum | solution.py:98
  1103.0 4.3 multiply_subtract_fusion
  (425 shorter events, 240.0 us)
Async XLA Ops:
  9.2 351.6 %all-gather.4.cloned.1.call-start = ((), (), s32[]{:S(2)}) async-start(), calls=%async_computation | async-start | bytes 2129920 | tf_op jit(solution)/shard_map/all_gather | solution.py:86
  18.1 636.9 %all-gather.6.cloned.1.call-start = ((), (), s32[]{:S(2)}) async-start(), calls=%async_computation.1 | async-start | bytes 2129920 | tf_op jit(solution)/shard_map/all_gather | solution.py:86
  373.5 74.5 %collective-permute-start.1 = (f32[256,128]{0,1:T(8,128)}, f32[256,128]{0,1:T(8,128)}, u32[]{:S(2)}, u32[]{:S(2)}) collective-permute-start(f32[256,128]{0,1:T(8,128)} %broadcast_select_fusion.11), channel_id=1, source_target_pairs={{0,1},{1,2},{2,3},{3,4},{4,5},{5,6},{6,7},{7,8},{8,9},{9,10},{10,1... | collective-permute-start | bytes 393224 | tf_op jit(solution)/shard_map/ppermute | solution.py:21
  374.7 74.8 %collective-permute-start.3 = (f32[256,128]{0,1:T(8,128)}, f32[256,128]{0,1:T(8,128)}, u32[]{:S(2)}, u32[]{:S(2)}) collective-permute-start(f32[256,128]{0,1:T(8,128)} %broadcast_select_fusion.10), channel_id=1, source_target_pairs={{0,64},{64,128},{128,192},{192,0},{1,65},{65,129},{129,193},{193,1... | collective-permute-start | bytes 393224 | tf_op jit(solution)/shard_map/ppermute | solution.py:21
  431.1 14.3 %collective-permute-start = (f32[256,128]{0,1:T(8,128)}, f32[256,128]{0,1:T(8,128)}, u32[]{:S(2)}, u32[]{:S(2)}) collective-permute-start(f32[256,128]{0,1:T(8,128)} %get-tuple-element.67), channel_id=1, source_target_pairs={{1,0},{2,1},{3,2},{4,3},{5,4},{6,5},{7,6},{8,7},{9,8},{10,9},{11,1... | collective-permute-start | bytes 393224 | tf_op jit(solution)/shard_map/ppermute | solution.py:23
  471.7 13.5 %collective-permute-start.7 = (f32[256,128]{0,1:T(8,128)S(1)}, f32[256,128]{0,1:T(8,128)S(1)}, u32[]{:S(2)}, u32[]{:S(2)}) collective-permute-start(f32[256,128]{0,1:T(8,128)S(1)} %get-tuple-element.59), channel_id=1, source_target_pairs={{64,0},{128,64},{192,128},{0,192},{65,1},{129,65},{193,129},{1,193... | collective-permute-start | bytes 393224 | tf_op jit(solution)/shard_map/ppermute | solution.py:23
  472.2 13.8 %collective-permute-start.5 = (f32[256,128]{0,1:T(8,128)S(1)}, f32[256,128]{0,1:T(8,128)S(1)}, u32[]{:S(2)}, u32[]{:S(2)}) collective-permute-start(f32[256,128]{0,1:T(8,128)S(1)} %get-tuple-element.61), channel_id=1, source_target_pairs={{1,0},{2,1},{3,2},{4,3},{5,4},{6,5},{7,6},{8,7},{9,8},{10,9},{11,1... | collective-permute-start | bytes 393224 | tf_op jit(solution)/shard_map/ppermute | solution.py:23
  483.0 12.9 %collective-permute-start.8 = (f32[256,128]{0,1:T(8,128)}, f32[256,128]{0,1:T(8,128)}, u32[]{:S(2)}, u32[]{:S(2)}) collective-permute-start(f32[256,128]{0,1:T(8,128)} %broadcast_select_fusion.8), channel_id=1, source_target_pairs={{0,64},{64,128},{128,192},{192,0},{1,65},{65,129},{129,193},{193,1... | collective-permute-start | bytes 393224 | tf_op jit(solution)/shard_map/ppermute | solution.py:21
  583.8 326.4 %all-gather.8.cloned.1.call-start = ((), (), s32[]{:S(2)}) async-start(), calls=%async_computation.2 | async-start | bytes 2129920 | tf_op jit(solution)/shard_map/all_gather | solution.py:86
  671.6 13.0 %collective-permute-start.12 = (f32[256,128]{0,1:T(8,128)}, f32[256,128]{0,1:T(8,128)S(1)}, u32[]{:S(2)}, u32[]{:S(2)}) collective-permute-start(f32[256,128]{0,1:T(8,128)} %get-tuple-element.53), channel_id=1, source_target_pairs={{64,0},{128,64},{192,128},{0,192},{65,1},{129,65},{193,129},{1,193... | collective-permute-start | bytes 393224 | tf_op jit(solution)/shard_map/ppermute | solution.py:23
  682.1 11.7 %collective-permute-start.11 = (f32[256,128]{0,1:T(8,128)}, f32[256,128]{0,1:T(8,128)}, u32[]{:S(2)}, u32[]{:S(2)}) collective-permute-start(f32[256,128]{0,1:T(8,128)} %broadcast_select_fusion.7), channel_id=1, source_target_pairs={{0,1},{1,2},{2,3},{3,4},{4,5},{5,6},{6,7},{7,8},{8,9},{9,10},{10,1... | collective-permute-start | bytes 393224 | tf_op jit(solution)/shard_map/ppermute | solution.py:21
  682.1 13.3 %collective-permute-start.13 = (f32[256,128]{0,1:T(8,128)}, f32[256,128]{0,1:T(8,128)}, u32[]{:S(2)}, u32[]{:S(2)}) collective-permute-start(f32[256,128]{0,1:T(8,128)} %broadcast_select_fusion.6), channel_id=1, source_target_pairs={{0,64},{64,128},{128,192},{192,0},{1,65},{65,129},{129,193},{193,1... | collective-permute-start | bytes 393224 | tf_op jit(solution)/shard_map/ppermute | solution.py:21
  683.9 12.4 %collective-permute-start.14 = (f32[2,256,128]{1,2,0:T(8,128)}, f32[2,256,128]{1,2,0:T(8,128)}, u32[]{:S(2)}, u32[]{:S(2)}) collective-permute-start(f32[2,256,128]{1,2,0:T(8,128)} %pad_maximum_fusion.2), channel_id=1, source_target_pairs={{0,32},{1,33},{2,34},{3,35},{4,36},{5,37},{6,38},{7,39},{8,40},{9,... | collective-permute-start | bytes 786440 | tf_op jit(solution)/shard_map/ppermute | solution.py:31
  731.1 12.0 %collective-permute-start.16 = (f32[256,128]{0,1:T(8,128)}, f32[256,128]{0,1:T(8,128)}, u32[]{:S(2)}, u32[]{:S(2)}) collective-permute-start(f32[256,128]{0,1:T(8,128)} %broadcast_select_fusion.5), channel_id=1, source_target_pairs={{0,1},{1,2},{2,3},{3,4},{4,5},{5,6},{6,7},{7,8},{8,9},{9,10},{10,1... | collective-permute-start | bytes 393224 | tf_op jit(solution)/shard_map/ppermute | solution.py:21
  731.1 13.5 %collective-permute-start.18 = (f32[256,128]{0,1:T(8,128)}, f32[256,128]{0,1:T(8,128)}, u32[]{:S(2)}, u32[]{:S(2)}) collective-permute-start(f32[256,128]{0,1:T(8,128)} %broadcast_select_fusion.4), channel_id=1, source_target_pairs={{0,64},{64,128},{128,192},{192,0},{1,65},{65,129},{129,193},{193,1... | collective-permute-start | bytes 393224 | tf_op jit(solution)/shard_map/ppermute | solution.py:21
  733.8 11.7 %collective-permute-start.19 = (f32[2,256,128]{1,2,0:T(8,128)}, f32[2,256,128]{1,2,0:T(8,128)}, u32[]{:S(2)}, u32[]{:S(2)}) collective-permute-start(f32[2,256,128]{1,2,0:T(8,128)} %pad_maximum_fusion.3), channel_id=1, source_target_pairs={{0,32},{1,33},{2,34},{3,35},{4,36},{5,37},{6,38},{7,39},{8,40},{9,... | collective-permute-start | bytes 786440 | tf_op jit(solution)/shard_map/ppermute | solution.py:31
  924.8 13.9 %collective-permute-start.22 = (f32[256,128]{0,1:T(8,128)}, f32[256,128]{0,1:T(8,128)S(1)}, u32[]{:S(2)}, u32[]{:S(2)}) collective-permute-start(f32[256,128]{0,1:T(8,128)} %get-tuple-element.41), channel_id=1, source_target_pairs={{64,0},{128,64},{192,128},{0,192},{65,1},{129,65},{193,129},{1,193... | collective-permute-start | bytes 393224 | tf_op jit(solution)/shard_map/ppermute | solution.py:23
  927.9 11.7 %collective-permute-start.20 = (f32[256,128]{0,1:T(8,128)}, f32[256,128]{0,1:T(8,128)}, u32[]{:S(2)}, u32[]{:S(2)}) collective-permute-start(f32[256,128]{0,1:T(8,128)} %get-tuple-element.43), channel_id=1, source_target_pairs={{1,0},{2,1},{3,2},{4,3},{5,4},{6,5},{7,6},{8,7},{9,8},{10,9},{11,1... | collective-permute-start | bytes 393224 | tf_op jit(solution)/shard_map/ppermute | solution.py:23
  937.6 11.7 %collective-permute-start.21 = (f32[256,128]{0,1:T(8,128)}, f32[256,128]{0,1:T(8,128)}, u32[]{:S(2)}, u32[]{:S(2)}) collective-permute-start(f32[256,128]{0,1:T(8,128)} %broadcast_select_fusion.3), channel_id=1, source_target_pairs={{0,1},{1,2},{2,3},{3,4},{4,5},{5,6},{6,7},{7,8},{8,9},{9,10},{10,1... | collective-permute-start | bytes 393224 | tf_op jit(solution)/shard_map/ppermute | solution.py:21
  937.6 14.0 %collective-permute-start.23 = (f32[256,128]{0,1:T(8,128)}, f32[256,128]{0,1:T(8,128)}, u32[]{:S(2)}, u32[]{:S(2)}) collective-permute-start(f32[256,128]{0,1:T(8,128)} %broadcast_select_fusion.2), channel_id=1, source_target_pairs={{0,64},{64,128},{128,192},{192,0},{1,65},{65,129},{129,193},{193,1... | collective-permute-start | bytes 393224 | tf_op jit(solution)/shard_map/ppermute | solution.py:21
  937.8 15.3 %collective-permute-start.24 = (f32[2,256,128]{1,2,0:T(8,128)S(1)}, f32[2,256,128]{1,2,0:T(8,128)S(1)}, u32[]{:S(2)}, u32[]{:S(2)}) collective-permute-start(f32[2,256,128]{1,2,0:T(8,128)S(1)} %pad_maximum_fusion.4), channel_id=1, source_target_pairs={{0,32},{1,33},{2,34},{3,35},{4,36},{5,37},{6,38},{7,39},{8,40},{9,... | collective-permute-start | bytes 786440 | tf_op jit(solution)/shard_map/ppermute | solution.py:31
  978.5 20.4 %collective-permute-start.26 = (f32[256,128]{0,1:T(8,128)}, f32[256,128]{0,1:T(8,128)}, u32[]{:S(2)}, u32[]{:S(2)}) collective-permute-start(f32[256,128]{0,1:T(8,128)} %broadcast_select_fusion.1), channel_id=1, source_target_pairs={{0,1},{1,2},{2,3},{3,4},{4,5},{5,6},{6,7},{7,8},{8,9},{9,10},{10,1... | collective-permute-start | bytes 393224 | tf_op jit(solution)/shard_map/ppermute | solution.py:21
  978.6 25.8 %collective-permute-start.28 = (f32[256,128]{0,1:T(8,128)}, f32[256,128]{0,1:T(8,128)}, u32[]{:S(2)}, u32[]{:S(2)}) collective-permute-start(f32[256,128]{0,1:T(8,128)} %broadcast_select_fusion), channel_id=1, source_target_pairs={{0,64},{64,128},{128,192},{192,0},{1,65},{65,129},{129,193},{193,1... | collective-permute-start | bytes 393224 | tf_op jit(solution)/shard_map/ppermute | solution.py:21
  984.3 26.3 %collective-permute-start.29 = (f32[2,256,128]{1,2,0:T(8,128)}, f32[2,256,128]{1,2,0:T(8,128)}, u32[]{:S(2)}, u32[]{:S(2)}) collective-permute-start(f32[2,256,128]{1,2,0:T(8,128)} %pad_maximum_fusion.5), channel_id=1, source_target_pairs={{0,32},{1,33},{2,34},{3,35},{4,36},{5,37},{6,38},{7,39},{8,40},{9,... | collective-permute-start | bytes 786440 | tf_op jit(solution)/shard_map/ppermute | solution.py:31
  (48 other events, 2358.9 us)
Sparse Core Ops, SparseCore 0:
  10.9 2.5 sort.21.cloned.1.call-done
  18.2 80.2 all-gather.3
  584.0 71.0 all-gather.5
  839.0 71.2 all-gather.7
  (1 shorter events, 0.0 us)
